TPU v7x, 32 devices: a whole 2x2x4 slice. The times are simulated.
32 devices in a mesh: dp: 2 (over y), fsdp: 16 (over z, x, core).
Axes of the slice: x: 2, y: 2, z: 4, core: 2. Of those that a mesh axis runs over, the one named last changes fastest.
Arguments:
- tokens: bfloat16 [32768, 768], P(('dp', 'fsdp')), may hold values from -6 to 6
- lengths: int32 [32], P(('dp', 'fsdp')), may hold values from 512 to 1024, as said below
- rand_blocks: int32 [32, 14, 12, 3], P(('dp', 'fsdp')), may hold values from 0 to 15
- cotangent: bfloat16 [32768, 768], P(('dp', 'fsdp')), may hold values from -6 to 6
- first_gain: bfloat16 [768], P(('dp', 'fsdp')), may hold values from 0.25 to 1.75
- first_shift: bfloat16 [768], P(('dp', 'fsdp')), may hold values from -1 to 1
- query_weight: bfloat16 [768, 768], P(('dp', 'fsdp')), may hold values from -0.4375 to 0.4375
- query_bias: bfloat16 [768], P(('dp', 'fsdp')), may hold values from -1 to 1
- key_weight: bfloat16 [768, 768], P(('dp', 'fsdp')), may hold values from -0.21875 to 0.21875
- value_weight: bfloat16 [768, 768], P(('dp', 'fsdp')), may hold values from -0.21875 to 0.21875
- value_bias: bfloat16 [768], P(('dp', 'fsdp')), may hold values from -1 to 1
- out_weight: bfloat16 [768, 768], P(('dp', 'fsdp')), may hold values from -0.875 to 0.875
- out_bias: bfloat16 [768], P(('dp', 'fsdp')), may hold values from -1 to 1
- second_gain: bfloat16 [768], P(('dp', 'fsdp')), may hold values from 0.25 to 1.75
- second_shift: bfloat16 [768], P(('dp', 'fsdp')), may hold values from -1 to 1
- up_weight: bfloat16 [768, 3072], P(('dp', 'fsdp')), may hold values from -0.21875 to 0.21875
- up_bias: bfloat16 [3072], P(('dp', 'fsdp')), may hold values from -1 to 1
- down_weight: bfloat16 [3072, 768], P(('dp', 'fsdp')), may hold values from -0.109375 to 0.109375
- down_bias: bfloat16 [768], P(('dp', 'fsdp')), may hold values from -1 to 1
Outputs:
- layer_out: bfloat16 [32768, 768], P(('dp', 'fsdp'))
- input_grad: float32 [32768, 768], P(('dp', 'fsdp'))
- first_gain_grad: float32 [768], P(('dp', 'fsdp'))
- first_shift_grad: float32 [768], P(('dp', 'fsdp'))
- query_weight_grad: float32 [768, 768], P(('dp', 'fsdp'))
- query_bias_grad: float32 [768], P(('dp', 'fsdp'))
- key_weight_grad: float32 [768, 768], P(('dp', 'fsdp'))
- value_weight_grad: float32 [768, 768], P(('dp', 'fsdp'))
- value_bias_grad: float32 [768], P(('dp', 'fsdp'))
- out_weight_grad: float32 [768, 768], P(('dp', 'fsdp'))
- out_bias_grad: float32 [768], P(('dp', 'fsdp'))
- second_gain_grad: float32 [768], P(('dp', 'fsdp'))
- second_shift_grad: float32 [768], P(('dp', 'fsdp'))
- up_weight_grad: float32 [768, 3072], P(('dp', 'fsdp'))
- up_bias_grad: float32 [3072], P(('dp', 'fsdp'))
- down_weight_grad: float32 [3072, 768], P(('dp', 'fsdp'))
- down_bias_grad: float32 [768], P(('dp', 'fsdp'))
Inputs may be any that keep to these rules, and one draw needn't show every extreme that they name: `lengths`: the live tokens of each window come first; the other slots of its 1024 are padding; some window has all 1024 live. `rand_blocks`: block numbers within the window.
All inputs are finite; a program needn't handle non-finite values.
Results may differ from a plain program's by a relative error of at most 0.02.
Values may be sent and summed in bfloat16 or wider, within the bound.
A program may use at most 256 MiB of HBM per device.

v0:
```python
import jax
import jax.numpy as jnp
from jax import lax
from jax.sharding import PartitionSpec as P

H = 12
HD = 64
BLK = 64
NBLK = 16


masked_fill = -1e30
bf_type = jnp.bfloat16
f_type = jnp.float32
highest = lax.Precision.HIGHEST


def layer_norm(values, gain, shift):
    centre = jnp.mean(values, axis=-1, keepdims=True)
    centred = values - centre
    inverse = lax.rsqrt(jnp.mean(centred * centred, axis=-1, keepdims=True) + 1e-05)
    return centred * inverse * gain + shift


def gelu_exact(values):
    return jax.nn.gelu(values, approximate=False)


def matmul(left, right):
    return jnp.dot(left, right, preferred_element_type=f_type)


def contract_rows(left, right):
    return jnp.einsum("ra,rb->ab", left, right, preferred_element_type=f_type)


def times_transpose(left, right):
    return jnp.einsum("ra,ba->rb", left, right, preferred_element_type=f_type)


def column_sums(values):
    return jnp.sum(values.astype(f_type), axis=0)


def log_total(scores):
    top = jnp.max(scores, axis=-1)
    return top + jnp.log(jnp.sum(jnp.exp(scores - top[..., None]), axis=-1))


def block_lists(rand_rows, count):
    later = jnp.arange(2, count, dtype=jnp.int32)
    fixed = jnp.stack(
        [jnp.zeros_like(later), jnp.ones_like(later), later - 1, later, later + 1], axis=-1
    )
    fixed = jnp.broadcast_to(fixed[:, None, :], (count - 2, rand_rows.shape[1], 5))
    return jnp.concatenate([fixed, rand_rows], axis=-1)


def selector(chosen, dtype):
    return (chosen[..., None] == jnp.arange(NBLK + 1, dtype=jnp.int32)[None, None, None, :]).astype(
        dtype
    )


def pick_blocks(key_heads, value_heads, length, chosen):
    spare = jnp.zeros((BLK, H, HD), key_heads.dtype)
    key_blocks = jnp.concatenate([key_heads, spare]).reshape(NBLK + 1, BLK, H, HD)
    value_blocks = jnp.concatenate([value_heads, spare]).reshape(NBLK + 1, BLK, H, HD)
    onehot = selector(chosen, bf_type)
    picked_keys = (
        jnp.einsum("bhjn,nkhd->bhjkd", onehot, key_blocks, preferred_element_type=f_type)
        .astype(bf_type)
        .reshape(NBLK - 2, H, 8 * BLK, HD)
    )
    picked_values = (
        jnp.einsum("bhjn,nkhd->bhjkd", onehot, value_blocks, preferred_element_type=f_type)
        .astype(bf_type)
        .reshape(NBLK - 2, H, 8 * BLK, HD)
    )
    offsets = jnp.arange(BLK, dtype=jnp.int32)
    picked_live = (chosen[..., None] * BLK + offsets[None, None, None, :] < length).reshape(
        NBLK - 2, H, 8 * BLK
    )
    return (picked_keys, picked_values, picked_live)


def global_scores_of(query_heads, key_heads, key_live):
    scores = jnp.einsum(
        "qhd,khd->hqk", query_heads[: 2 * BLK], key_heads, preferred_element_type=f_type
    )
    return jnp.where(key_live[None, None, :], scores, masked_fill)


def block_scores_of(query_heads, picked_keys, picked_live):
    block_query = query_heads[2 * BLK :].reshape(NBLK - 2, BLK, H, HD)
    scores = jnp.einsum("bqhd,bhkd->bhqk", block_query, picked_keys, preferred_element_type=f_type)
    return (jnp.where(picked_live[:, :, None, :], scores, masked_fill), block_query)


def attend(query_heads, key_heads, value_heads, key_live, length, chosen):
    token_count = query_heads.shape[0]
    global_scores = global_scores_of(query_heads, key_heads, key_live)
    global_log = log_total(global_scores)
    global_probs = jnp.exp(global_scores - global_log[..., None]).astype(bf_type)
    global_out = jnp.einsum(
        "hqk,khd->qhd", global_probs, value_heads, preferred_element_type=f_type
    )
    picked_keys, picked_values, picked_live = pick_blocks(key_heads, value_heads, length, chosen)
    block_scores, block_query = block_scores_of(query_heads, picked_keys, picked_live)
    block_log = log_total(block_scores)
    block_probs = jnp.exp(block_scores - block_log[..., None]).astype(bf_type)
    block_out = jnp.einsum(
        "bhqk,bhkd->bqhd", block_probs, picked_values, preferred_element_type=f_type
    )
    joined = jnp.concatenate([global_out, block_out.reshape(token_count - 2 * BLK, H, HD)])
    return (joined, global_log, block_log)


def attend_back(
    query_heads, key_heads, value_heads, key_live, length, chosen, global_log, block_log, grad_heads
):
    token_count = query_heads.shape[0]
    front = 2 * BLK
    global_scores = global_scores_of(query_heads, key_heads, key_live)
    global_probs = jnp.exp(global_scores - global_log[..., None])
    global_dprob = jnp.einsum(
        "qhd,khd->hqk", grad_heads[:front], value_heads, preferred_element_type=f_type
    )
    global_delta = jnp.sum(global_probs * global_dprob, axis=-1, keepdims=True)
    global_dscore = (global_probs * (global_dprob - global_delta)).astype(bf_type)
    query_front = jnp.einsum(
        "hqk,khd->qhd", global_dscore, key_heads, preferred_element_type=f_type
    )
    key_grad = jnp.einsum(
        "hqk,qhd->khd", global_dscore, query_heads[:front], preferred_element_type=f_type
    )
    value_grad = jnp.einsum(
        "hqk,qhd->khd",
        global_probs.astype(bf_type),
        grad_heads[:front],
        preferred_element_type=f_type,
    )
    picked_keys, picked_values, picked_live = pick_blocks(key_heads, value_heads, length, chosen)
    block_scores, block_query = block_scores_of(query_heads, picked_keys, picked_live)
    block_probs = jnp.exp(block_scores - block_log[..., None])
    block_grad = grad_heads[front:].reshape(NBLK - 2, BLK, H, HD)
    block_dprob = jnp.einsum(
        "bqhd,bhkd->bhqk", block_grad, picked_values, preferred_element_type=f_type
    )
    block_delta = jnp.sum(block_probs * block_dprob, axis=-1, keepdims=True)
    block_dscore = (block_probs * (block_dprob - block_delta)).astype(bf_type)
    query_rest = jnp.einsum(
        "bhqk,bhkd->bqhd", block_dscore, picked_keys, preferred_element_type=f_type
    )
    picked_key_grad = jnp.einsum(
        "bhqk,bqhd->bhkd", block_dscore, block_query, preferred_element_type=f_type
    )
    picked_value_grad = jnp.einsum(
        "bhqk,bqhd->bhkd", block_probs.astype(bf_type), block_grad, preferred_element_type=f_type
    )
    onehot = selector(chosen, f_type)
    key_back = jnp.einsum(
        "bhjn,bhjkd->nkhd",
        onehot,
        picked_key_grad.reshape(NBLK - 2, H, 8, BLK, HD),
        precision=highest,
    )
    value_back = jnp.einsum(
        "bhjn,bhjkd->nkhd",
        onehot,
        picked_value_grad.reshape(NBLK - 2, H, 8, BLK, HD),
        precision=highest,
    )
    key_back = key_back.reshape((NBLK + 1) * BLK, H, HD)[:token_count]
    value_back = value_back.reshape((NBLK + 1) * BLK, H, HD)[:token_count]
    query_grad = jnp.concatenate([query_front, query_rest.reshape(token_count - front, H, HD)])
    return (query_grad, key_grad + key_back, value_grad + value_back)


def forward_window(weights, window, length, rand_rows):
    (
        first_gain,
        first_shift,
        query_weight,
        query_bias,
        key_weight,
        value_weight,
        value_bias,
        out_weight,
        out_bias,
        second_gain,
        second_shift,
        up_weight,
        up_bias,
        down_weight,
        down_bias,
    ) = weights
    token_count, feature_width = window.shape
    inputs = window.astype(f_type)
    key_live = jnp.arange(token_count) < length
    chosen = block_lists(rand_rows, NBLK)
    normed = layer_norm(inputs, first_gain.astype(f_type), first_shift.astype(f_type)).astype(
        bf_type
    )
    query_flat = ((matmul(normed, query_weight) + query_bias.astype(f_type)) * 0.125).astype(
        bf_type
    )
    key_flat = matmul(normed, key_weight).astype(bf_type)
    value_flat = (matmul(normed, value_weight) + value_bias.astype(f_type)).astype(bf_type)
    joined, global_log, block_log = attend(
        query_flat.reshape(token_count, H, HD),
        key_flat.reshape(token_count, H, HD),
        value_flat.reshape(token_count, H, HD),
        key_live,
        length,
        chosen,
    )
    mixed = joined.reshape(token_count, feature_width).astype(bf_type)
    residual = inputs + matmul(mixed, out_weight) + out_bias.astype(f_type)
    normed_two = layer_norm(
        residual, second_gain.astype(f_type), second_shift.astype(f_type)
    ).astype(bf_type)
    hidden = matmul(normed_two, up_weight) + up_bias.astype(f_type)
    activated = gelu_exact(hidden).astype(bf_type)
    result = (residual + matmul(activated, down_weight) + down_bias.astype(f_type)).astype(bf_type)
    kept = (
        normed,
        query_flat,
        key_flat,
        value_flat,
        global_log,
        block_log,
        mixed,
        residual,
        normed_two,
        hidden,
        activated,
    )
    return (result, kept)


def feed_back(weights, grad_window, kept):
    (
        first_gain,
        first_shift,
        query_weight,
        query_bias,
        key_weight,
        value_weight,
        value_bias,
        out_weight,
        out_bias,
        second_gain,
        second_shift,
        up_weight,
        up_bias,
        down_weight,
        down_bias,
    ) = weights
    (
        normed,
        query_flat,
        key_flat,
        value_flat,
        global_log,
        block_log,
        mixed,
        residual,
        normed_two,
        hidden,
        activated,
    ) = kept
    grad_out = grad_window.astype(f_type)
    grad_branch = grad_out.astype(bf_type)
    down_grad = contract_rows(activated, grad_branch)
    down_bias_grad = column_sums(grad_branch)
    grad_act = times_transpose(grad_branch, down_weight)
    unused, gelu_back = jax.vjp(gelu_exact, hidden)
    grad_hidden = gelu_back(grad_act)[0].astype(bf_type)
    up_grad = contract_rows(normed_two, grad_hidden)
    up_bias_grad = column_sums(grad_hidden)
    grad_normed_two = times_transpose(grad_hidden, up_weight)
    unused, norm_back_two = jax.vjp(
        layer_norm, residual, second_gain.astype(f_type), second_shift.astype(f_type)
    )
    grad_resid_norm, second_gain_grad, second_shift_grad = norm_back_two(grad_normed_two)
    grad_resid = grad_out + grad_resid_norm
    grads = (second_gain_grad, second_shift_grad, up_grad, up_bias_grad, down_grad, down_bias_grad)
    return (grad_resid, grads)


def attention_back(weights, window, length, rand_rows, grad_resid, kept):
    (
        first_gain,
        first_shift,
        query_weight,
        query_bias,
        key_weight,
        value_weight,
        value_bias,
        out_weight,
        out_bias,
        second_gain,
        second_shift,
        up_weight,
        up_bias,
        down_weight,
        down_bias,
    ) = weights
    (
        normed,
        query_flat,
        key_flat,
        value_flat,
        global_log,
        block_log,
        mixed,
        residual,
        normed_two,
        hidden,
        activated,
    ) = kept
    token_count, feature_width = window.shape
    inputs = window.astype(f_type)
    key_live = jnp.arange(token_count) < length
    chosen = block_lists(rand_rows, NBLK)
    grad_attn = grad_resid.astype(bf_type)
    out_grad = contract_rows(mixed, grad_attn)
    out_bias_grad = column_sums(grad_attn)
    grad_mixed = times_transpose(grad_attn, out_weight).astype(bf_type).reshape(token_count, H, HD)
    query_grad_heads, key_grad_heads, value_grad_heads = attend_back(
        query_flat.reshape(token_count, H, HD),
        key_flat.reshape(token_count, H, HD),
        value_flat.reshape(token_count, H, HD),
        key_live,
        length,
        chosen,
        global_log,
        block_log,
        grad_mixed,
    )
    grad_query = query_grad_heads.reshape(token_count, feature_width).astype(bf_type)
    grad_key = key_grad_heads.reshape(token_count, feature_width).astype(bf_type)
    grad_value = value_grad_heads.reshape(token_count, feature_width).astype(bf_type)
    query_grad = contract_rows(normed, grad_query) * 0.125
    query_bias_grad = column_sums(grad_query) * 0.125
    key_grad = contract_rows(normed, grad_key)
    value_grad = contract_rows(normed, grad_value)
    value_bias_grad = column_sums(grad_value)
    grad_normed = (
        times_transpose(grad_query, query_weight) * 0.125
        + times_transpose(grad_key, key_weight)
        + times_transpose(grad_value, value_weight)
    )
    unused, norm_back_one = jax.vjp(
        layer_norm, inputs, first_gain.astype(f_type), first_shift.astype(f_type)
    )
    grad_input_norm, first_gain_grad, first_shift_grad = norm_back_one(grad_normed)
    grad_inputs = grad_resid + grad_input_norm
    grads = (
        first_gain_grad,
        first_shift_grad,
        query_grad,
        query_bias_grad,
        key_grad,
        value_grad,
        value_bias_grad,
        out_grad,
        out_bias_grad,
    )
    return (grad_inputs, grads)


def body(
    tokens,
    lengths,
    rand_blocks,
    cotangent,
    first_gain,
    first_shift,
    query_weight,
    query_bias,
    key_weight,
    value_weight,
    value_bias,
    out_weight,
    out_bias,
    second_gain,
    second_shift,
    up_weight,
    up_bias,
    down_weight,
    down_bias,
):
    shards = (
        first_gain,
        first_shift,
        query_weight,
        query_bias,
        key_weight,
        value_weight,
        value_bias,
        out_weight,
        out_bias,
        second_gain,
        second_shift,
        up_weight,
        up_bias,
        down_weight,
        down_bias,
    )
    whole = (
        lax.all_gather(shards[0], ("dp", "fsdp"), axis=0, tiled=True),
        lax.all_gather(shards[1], ("dp", "fsdp"), axis=0, tiled=True),
        lax.all_gather(shards[2], ("dp", "fsdp"), axis=0, tiled=True),
        lax.all_gather(shards[3], ("dp", "fsdp"), axis=0, tiled=True),
        lax.all_gather(shards[4], ("dp", "fsdp"), axis=0, tiled=True),
        lax.all_gather(shards[5], ("dp", "fsdp"), axis=0, tiled=True),
        lax.all_gather(shards[6], ("dp", "fsdp"), axis=0, tiled=True),
        lax.all_gather(shards[7], ("dp", "fsdp"), axis=0, tiled=True),
        lax.all_gather(shards[8], ("dp", "fsdp"), axis=0, tiled=True),
        lax.all_gather(shards[9], ("dp", "fsdp"), axis=0, tiled=True),
        lax.all_gather(shards[10], ("dp", "fsdp"), axis=0, tiled=True),
        lax.all_gather(shards[11], ("dp", "fsdp"), axis=0, tiled=True),
        lax.all_gather(shards[12], ("dp", "fsdp"), axis=0, tiled=True),
        lax.all_gather(shards[13], ("dp", "fsdp"), axis=0, tiled=True),
        lax.all_gather(shards[14], ("dp", "fsdp"), axis=0, tiled=True),
    )
    window_count = lengths.shape[0]
    feature_width = tokens.shape[1]
    slot_count = tokens.shape[0] // window_count
    token_windows = tokens.reshape(window_count, slot_count, feature_width)
    cot_windows = cotangent.reshape(window_count, slot_count, feature_width)

    def forward_turn(counter, window_items):
        window, length, rand_rows = window_items
        result, kept = forward_window(whole, window, length, rand_rows)
        return (counter, (result, kept))

    unused, (results, kept_all) = lax.scan(
        forward_turn, jnp.zeros((), jnp.int32), (token_windows, lengths, rand_blocks)
    )

    def add_up(totals, grads):
        return tuple((total + piece for total, piece in zip(totals, grads)))

    feed_start = tuple((jnp.zeros(item.shape, f_type) for item in whole[9:]))
    attention_start = tuple((jnp.zeros(item.shape, f_type) for item in whole[:9]))

    def backward_turn(totals, window_items):
        window, length, rand_rows, grad_window, kept = window_items
        grad_resid, feed_grads = feed_back(whole, grad_window, kept)
        grad_inputs, attention_grads = attention_back(
            whole, window, length, rand_rows, grad_resid, kept
        )
        return (add_up(totals, attention_grads + feed_grads), grad_inputs)

    totals, grad_inputs = lax.scan(
        backward_turn,
        attention_start + feed_start,
        (token_windows, lengths, rand_blocks, cot_windows, kept_all),
    )
    owned = lax.psum_scatter(totals, ("dp", "fsdp"), scatter_dimension=0, tiled=True)
    all_owned = tuple(owned)
    layer_out = results.reshape(window_count * slot_count, feature_width)
    input_grad = grad_inputs.reshape(window_count * slot_count, feature_width)
    return (
        layer_out,
        input_grad,
        all_owned[0],
        all_owned[1],
        all_owned[2],
        all_owned[3],
        all_owned[4],
        all_owned[5],
        all_owned[6],
        all_owned[7],
        all_owned[8],
        all_owned[9],
        all_owned[10],
        all_owned[11],
        all_owned[12],
        all_owned[13],
        all_owned[14],
    )


def solution(mesh):
    in_specs = (
        P(("dp", "fsdp"), None),
        P(("dp", "fsdp")),
        P(("dp", "fsdp"), None, None, None),
        P(("dp", "fsdp"), None),
        P(("dp", "fsdp")),
        P(("dp", "fsdp")),
        P(("dp", "fsdp"), None),
        P(("dp", "fsdp")),
        P(("dp", "fsdp"), None),
        P(("dp", "fsdp"), None),
        P(("dp", "fsdp")),
        P(("dp", "fsdp"), None),
        P(("dp", "fsdp")),
        P(("dp", "fsdp")),
        P(("dp", "fsdp")),
        P(("dp", "fsdp"), None),
        P(("dp", "fsdp")),
        P(("dp", "fsdp"), None),
        P(("dp", "fsdp")),
    )
    out_specs = (
        P(("dp", "fsdp"), None),
        P(("dp", "fsdp"), None),
        P(("dp", "fsdp")),
        P(("dp", "fsdp")),
        P(("dp", "fsdp"), None),
        P(("dp", "fsdp")),
        P(("dp", "fsdp"), None),
        P(("dp", "fsdp"), None),
        P(("dp", "fsdp")),
        P(("dp", "fsdp"), None),
        P(("dp", "fsdp")),
        P(("dp", "fsdp")),
        P(("dp", "fsdp")),
        P(("dp", "fsdp"), None),
        P(("dp", "fsdp")),
        P(("dp", "fsdp"), None),
        P(("dp", "fsdp")),
    )
    return jax.shard_map(body, mesh=mesh, in_specs=in_specs, out_specs=out_specs, check_vma=False)
```

profile of v0, /device:TPU:0, one launch (start us, length us, event | category | flops | bytes accessed | tf_op | source)
XLA Modules:
  0.0 1212.5 jit_solution(7680123746888792455)
XLA Ops:
  19.5 43.0 %all-reduce.21 = (bf16[768]{0:T(1024)(128)(2,1)S(1)}, bf16[768]{0:T(1024)(128)(2,1)S(1)}, bf16[768]{0:T(1024)(128)(2,1)S(1)}, bf16[768]{0:T(1024)(128)(2,1)S(1)}...) all-reduce(bf16[768]{0:T(1024)(128)(2,1)S(1)} %dynamic-update-slice, ...), channel_id=1, replica_groups=mesh['dp'=2,'fsdp'=16] {'dp','fsdp'}, use_global_device_ids=true, to_apply=%add.6 | all-reduce | flops 9216 | bytes 36864
  69.4 2.9 multiply_convert_fusion.3
  73.1 3.4 reshape.370
  76.5 46.8 %all-gather.11.cloned.1.call-done = bf16[768,768]{1,0:T(8,128)(2,1)} async-done(((bf16[24,768]{1,0:T(8,128)(2,1)}), bf16[768,768]{1,0:T(8,128)(2,1)}) %all-gather.11.cloned.1.call-update) | async-done | bytes 1179664 | tf_op jit(solution)/shard_map/all_gather | solution.py:417
  123.3 2.9 convolution_convert_fusion.1
  126.2 2.9 copy.94
  129.1 50.0 %all-gather.7.cloned.1.call-done = bf16[768,768]{1,0:T(8,128)(2,1)} async-done(((bf16[24,768]{1,0:T(8,128)(2,1)}), bf16[768,768]{1,0:T(8,128)(2,1)}) %all-gather.7.cloned.1.call-update) | async-done | bytes 1179664 | tf_op jit(solution)/shard_map/all_gather | solution.py:418
  179.0 4.0 add_convert_fusion.3
  183.0 4.6 copy.87
  194.3 2.5 concatenate.43
  196.8 16.1 %convert_bitcast_fusion.1 = bf16[14,12,8,64,64]{4,0,2,3,1:T(8,128)(2,1)} fusion(bf16[17,64,12,64,1]{3,1,0,2,4:T(8,128)(2,1)} %bitcast.140, pred[14,12,8,17,1]{3,2,1,0,4:T(8,128)(4,1)S(1)} %fusion.41), kind=kOutput, calls=%fused_computation.5 | convolution fusion | flops 192675840 | bytes 12704064 | tf_op jit(solution)/shard_map/while/body/eval_jaxpr/bhjn,nkhd->bhjkd/dot_general | solution.py:76
  212.9 38.9 %copy.92 = bf16[14,12,8,64,64]{3,2,4,1,0:T(8,128)(2,1)} copy(bf16[14,12,8,64,64]{4,0,2,3,1:T(8,128)(2,1)} %convert_bitcast_fusion.1) | data formatting | bytes 22020096 | tf_op jit(solution)/shard_map/while/body/eval_jaxpr/convert_element_type | solution.py:77
  251.7 29.2 %reshape.369 = bf16[14,12,512,64]{2,3,1,0:T(8,128)(2,1)} reshape(bf16[14,12,8,64,64]{3,2,4,1,0:T(8,128)(2,1)} %copy.92) | data formatting | bytes 22020096 | tf_op jit(solution)/shard_map/while/body/eval_jaxpr/reshape | solution.py:78
  280.9 4.4 concatenate.45
  285.3 16.3 %convert_bitcast_fusion = bf16[14,12,8,64,64]{4,0,2,3,1:T(8,128)(2,1)} fusion(bf16[17,64,12,64,1]{3,1,0,2,4:T(8,128)(2,1)} %bitcast.139, pred[14,12,8,17,1]{3,2,1,0,4:T(8,128)(4,1)S(1)} %fusion.41), kind=kOutput, calls=%fused_computation.4 | convolution fusion | flops 192675840 | bytes 12704064 | tf_op jit(solution)/shard_map/while/body/eval_jaxpr/bhjn,nkhd->bhjkd/dot_general | solution.py:71
  301.6 38.8 %copy.97 = bf16[14,12,8,64,64]{3,2,4,1,0:T(8,128)(2,1)} copy(bf16[14,12,8,64,64]{4,0,2,3,1:T(8,128)(2,1)} %convert_bitcast_fusion) | data formatting | bytes 22020096 | tf_op jit(solution)/shard_map/while/body/eval_jaxpr/convert_element_type | solution.py:72
  340.4 29.5 %reshape.372 = bf16[14,12,512,64]{2,3,1,0:T(8,128)(2,1)} reshape(bf16[14,12,8,64,64]{3,2,4,1,0:T(8,128)(2,1)} %copy.97) | data formatting | bytes 22020096 | tf_op jit(solution)/shard_map/while/body/eval_jaxpr/reshape | solution.py:73
  369.9 16.9 %select_reduce_fusion = (f32[14,12,64]{2,1,0:T(8,128)S(1)}, f32[14,12,64,512]{3,2,1,0:T(8,128)}) fusion(pred[14,12,512]{2,1,0:T(8,128)(4,1)S(1)} %copy.93, bf16[14,12,512,64]{2,3,1,0:T(8,128)(2,1)} %reshape.372, bf16[14,64,12,64]{1,0,3,2:T(8,128)(2,1)} %reshape.370), kind=kOutput, calls=%fused_computation.10 | convolution fusion | flops 715642368 | bytes 34535424 | tf_op jit(solution)/shard_map/while/body/eval_jaxpr/bqhd,bhkd->bhqk/dot_general | solution.py:96
  386.8 10.6 exponential_reduce_fusion
  397.5 14.6 %convert_bitcast_fusion.3 = bf16[14,64,12,64]{1,3,2,0:T(8,128)(2,1)} fusion(bf16[14,12,512,64]{2,3,1,0:T(8,128)(2,1)} %reshape.369, f32[14,12,64,512]{3,2,1,0:T(8,128)} %get-tuple-element.316, f32[14,12,64]{2,1,0:T(8,128)S(1)} %log_add_fusion, pred[14,12,512]{2,1,0:T(8,128)(4,1)S(1)} %copy.93), kind=kOutput, calls=%fused_computation.76 | convolution fusion | flops 721846272 | bytes 34535424 | tf_op jit(solution)/shard_map/while/body/eval_jaxpr/bhqk,bhkd->bqhd/dot_general | solution.py:112
  412.1 5.5 copy.99
  417.6 4.4 concatenate.46
  422.1 3.4 fusion.75
  427.6 38.2 %multiply_convert_fusion.1 = (bf16[1024,3072]{1,0:T(8,128)(2,1)}, f32[1024,3072]{1,0:T(8,128)}, f32[1024,3072]{1,0:T(8,128)}) fusion(f32[3072]{0:T(1024)S(1)} %convert_element_type.199, bf16[768,3072]{1,0:T(8,128)(2,1)} %all-gather.15.cloned.1.call-done, f32[1024,768]{0,1:T(8,128)} %copy-done.5, f32[768]{0:T(1024)S(1)} %convert_element_type.197, ...), kind=kOutput, calls=%fused_computation.16 | convolution fusion | flops 5043388416 | bytes 39348224 | tf_op jit(solution)/shard_map/while/body/eval_jaxpr/dot_general | solution.py:30
  465.8 17.4 %convert_reduce_fusion = (f32[3072]{0:T(1024)}, bf16[1024,3072]{1,0:T(8,128)(2,1)}) fusion(f32[1024,3072]{1,0:T(8,128)} %get-tuple-element.310, bf16[1024,768]{1,0:T(8,128)(2,1)S(1)} %copy-done.30, bf16[3072,768]{1,0:T(8,128)(2,1)} %all-gather.17.cloned.1.call-done, f32[1024,3072]{1,0:T(8,128)} %get-tuple-element.321, f32[3072]{0:T(1024)S(1)} %convert_element_type.199), kind=kOutput, calls=%fused_computation.14 | convolution fusion | flops 4885312512 | bytes 37773312 | tf_op jit(solution)/shard_map/while/body/eval_jaxpr/ra,ba->rb/dot_general | solution.py:38
  483.2 10.8 fusion.76
  494.0 3.7 copy.102
  497.7 3.5 multiply_reduce_fusion.2
  504.6 2.8 fusion.39
  509.8 3.6 reshape.373
  513.4 24.7 %multiply_reduce_fusion = (f32[14,12,64]{2,1,0:T(8,128)S(1)}, f32[14,12,64,512]{3,2,1,0:T(8,128)}) fusion(f32[14,12,64,512]{3,2,1,0:T(8,128)} %get-tuple-element.316, f32[14,12,64]{2,1,0:T(8,128)S(1)} %copy-done.21, pred[14,12,512]{2,1,0:T(8,128)(4,1)S(1)} %copy-done.19, bf16[14,12,512,64]{2,3,1,0:T(8,128)(2,1)} %reshape.369, ...), kind=kOutput, calls=%fused_computation.7 | convolution fusion | flops 726652416 | bytes 56598528 | tf_op jit(solution)/shard_map/while/body/eval_jaxpr/bqhd,bhkd->bhqk/dot_general | solution.py:147
  538.1 19.3 %multiply_convert_fusion = bf16[14,12,64,512]{3,2,1,0:T(8,128)(2,1)} fusion(f32[14,12,64,512]{3,2,1,0:T(8,128)} %get-tuple-element.323, f32[14,12,64,512]{3,2,1,0:T(8,128)} %get-tuple-element.316, f32[14,12,64]{2,1,0:T(8,128)S(1)} %get-tuple-element.322, f32[14,12,64]{2,1,0:T(8,128)S(1)} %copy-done.21, pred[14,12,512]{2,1,0:T(8,128)(4,1)S(1)} %copy-done.19), kind=kLoop, calls=%fused_computation.6 | loop fusion | flops 27525120 | bytes 55222272 | tf_op jit(solution)/shard_map/while/body/eval_jaxpr/convert_element_type | solution.py:151
  557.4 7.4 convert_bitcast_fusion.2
  564.8 3.8 copy.104
  568.7 4.6 concatenate.49
  573.3 4.8 multiply_reduce_fusion.1
  584.0 3.1 convolution_multiply_fusion
  587.1 15.5 %fusion.34 = f32[14,12,512,64]{2,3,1,0:T(8,128)} fusion(bf16[14,12,64,512]{3,2,1,0:T(8,128)(2,1)} %multiply_convert_fusion, bf16[14,64,12,64]{1,0,3,2:T(8,128)(2,1)} %reshape.370), kind=kOutput, calls=%fused_computation.83 | convolution fusion | flops 704643072 | bytes 34406400 | tf_op jit(solution)/shard_map/while/body/eval_jaxpr/bhqk,bqhd->bhkd/dot_general | solution.py:155
  602.6 32.5 %reshape.374 = f32[14,12,8,64,64]{3,2,4,1,0:T(8,128)} reshape(f32[14,12,512,64]{2,3,1,0:T(8,128)} %fusion.34) | data formatting | bytes 44040192 | tf_op jit(solution)/shard_map/while/body/eval_jaxpr/reshape | solution.py:165
  635.1 25.1 %fusion.2 = f32[12,64,64,17,1]{1,3,0,2,4:T(8,128)} fusion(f32[14,12,8,64,64]{3,2,4,1,0:T(8,128)} %reshape.374, s32[14,12,8]{2,1,0:T(8,128)S(1)} %copy-done.23), kind=kOutput, calls=%fused_computation.2 | convolution fusion | flops 1123047680 | bytes 25367808 | tf_op jit(solution)/shard_map/while/body/eval_jaxpr/bhjn,bhjkd->nkhd/dot_general | solution.py:162
  660.3 4.8 copy.162
  665.1 3.2 slice.60
  668.3 6.4 slice.53
  674.7 3.4 fusion.27
  679.3 3.1 fusion.65
  682.4 15.8 %fusion.30 = f32[14,12,512,64]{2,3,1,0:T(8,128)} fusion(bf16[14,64,12,64]{1,0,3,2:T(8,128)(2,1)} %reshape.373, f32[14,12,64,512]{3,2,1,0:T(8,128)} %get-tuple-element.316, f32[14,12,64]{2,1,0:T(8,128)S(1)} %copy-done.21, pred[14,12,512]{2,1,0:T(8,128)(4,1)S(1)} %copy-done.19), kind=kOutput, calls=%fused_computation.79 | convolution fusion | flops 721158144 | bytes 45545472 | tf_op jit(solution)/shard_map/while/body/eval_jaxpr/bhqk,bqhd->bhkd/dot_general | solution.py:158
  698.2 32.3 %reshape.375 = f32[14,12,8,64,64]{3,2,4,1,0:T(8,128)} reshape(f32[14,12,512,64]{2,3,1,0:T(8,128)} %fusion.30) | data formatting | bytes 44040192 | tf_op jit(solution)/shard_map/while/body/eval_jaxpr/reshape | solution.py:171
  730.5 25.2 %fusion = f32[12,64,64,17,1]{1,3,0,2,4:T(8,128)} fusion(f32[14,12,8,64,64]{3,2,4,1,0:T(8,128)} %reshape.375, s32[14,12,8]{2,1,0:T(8,128)S(1)} %copy-done.23), kind=kOutput, calls=%fused_computation | convolution fusion | flops 1123047680 | bytes 25367808 | tf_op jit(solution)/shard_map/while/body/eval_jaxpr/bhjn,bhjkd->nkhd/dot_general | solution.py:168
  755.7 4.5 copy.161
  760.3 3.3 slice.61
  763.5 6.4 slice.55
  769.9 5.4 convert_reduce_fusion.4
  776.5 3.1 fusion.63
  779.7 10.6 fusion.61
  791.7 10.3 fusion.77
  802.7 10.1 add_convert_fusion.1
  812.8 2.7 copy.111
  815.9 3.3 fusion.78
  824.9 3.2 convert_reduce_fusion.2
  828.1 40.3 %all-reduce.20 = (f32[768]{0:T(1024)S(1)}, f32[768]{0:T(1024)S(1)}, f32[768]{0:T(1024)S(1)}, f32[768]{0:T(1024)S(1)}, f32[768]{0:T(1024)S(1)}, /*index=5*/f32[76...) all-reduce(f32[768]{0:T(1024)S(1)} %get-tuple-element.243, ...), channel_id=2, replica_groups=mesh['dp'=2,'fsdp'=16] {'dp','fsdp'}, use_global_device_ids=true, to_apply=%region_15.16.clone | all-reduce | flops 9216 | bytes 73728
  873.1 3.5 copy.112
  877.3 45.0 %reduce-scatter.11.cloned.1.call-done = f32[24,768]{1,0:T(8,128)} async-done(((f32[768,768]{1,0:T(8,128)}), f32[24,768]{1,0:T(8,128)}) %reduce-scatter.11.cloned.1.call-update) | async-done | bytes 73744 | tf_op jit(solution)/shard_map/reduce_scatter | solution.py:463
  922.2 141.8 %reduce-scatter.15.cloned.1.call-done = f32[24,3072]{1,0:T(8,128)} async-done(((f32[768,3072]{1,0:T(8,128)}), f32[24,3072]{1,0:T(8,128)}) %reduce-scatter.15.cloned.1.call-update) | async-done | bytes 294928 | tf_op jit(solution)/shard_map/reduce_scatter | solution.py:463
  1064.0 141.5 %reduce-scatter.17.cloned.1.call-done = f32[96,768]{1,0:T(8,128)} async-done(((f32[3072,768]{1,0:T(8,128)}), f32[96,768]{1,0:T(8,128)}) %reduce-scatter.17.cloned.1.call-update) | async-done | bytes 294928 | tf_op jit(solution)/shard_map/reduce_scatter | solution.py:463
  (271 shorter events, 55.1 us)
Async XLA Ops:
  7.2 57.8 %copy-start.28 = (bf16[1024,768]{1,0:T(8,128)(2,1)S(1)}, bf16[1024,768]{1,0:T(8,128)(2,1)}, u32[]{:S(2)}) copy-start(bf16[1024,768]{1,0:T(8,128)(2,1)} %param.19) | copy-start | bytes 4718596
  7.2 62.2 %all-gather.9.cloned.1.call-start = ((), (), s32[]{:S(2)}) async-start(), calls=%async_computation.7 | async-start | bytes 1216512 | tf_op jit(solution)/shard_map/all_gather | solution.py:415
  7.9 115.4 %all-gather.11.cloned.1.call-start = ((), (), s32[]{:S(2)}) async-start(), calls=%async_computation.8 | async-start | bytes 1216512 | tf_op jit(solution)/shard_map/all_gather | solution.py:417
  8.7 170.3 %all-gather.7.cloned.1.call-start = ((), (), s32[]{:S(2)}) async-start(), calls=%async_computation.6 | async-start | bytes 1216512 | tf_op jit(solution)/shard_map/all_gather | solution.py:418
  9.4 412.6 %all-gather.13.cloned.1.call-start = ((), (), s32[]{:S(2)}) async-start(), calls=%async_computation.9 | async-start | bytes 1216512 | tf_op jit(solution)/shard_map/all_gather | solution.py:420
  10.0 417.6 %all-gather.15.cloned.1.call-start = ((), (), s32[]{:S(2)}) async-start(), calls=%async_computation.10 | async-start | bytes 4866048 | tf_op jit(solution)/shard_map/all_gather | solution.py:424
  10.6 455.3 %all-gather.17.cloned.1.call-start = ((), (), s32[]{:S(2)}) async-start(), calls=%async_computation.11 | async-start | bytes 4866048 | tf_op jit(solution)/shard_map/all_gather | solution.py:426
  11.2 866.1 %reduce-scatter.13.cloned.1.call-start = ((), (), s32[]{:S(2)}) async-start(), calls=%async_computation.15 | async-start | bytes 2433024 | tf_op jit(solution)/shard_map/reduce_scatter | solution.py:463
  11.9 179.2 %copy-start.56 = (pred[1024]{0:T(1024)(128)(4,1)}, pred[1024]{0:T(1024)(128)(4,1)S(1)}, u32[]{:S(2)}) copy-start(pred[1024]{0:T(1024)(128)(4,1)S(1)} %iota_compare_fusion.1) | copy-start | bytes 3076
  62.5 116.5 %copy-start.42 = (f32[768]{0:T(1024)}, f32[768]{0:T(1024)S(1)}, u32[]{:S(2)}) copy-start(f32[768]{0:T(1024)S(1)} %convert_element_type.181) | copy-start | bytes 9220
  62.5 116.5 %copy-start.63 = (f32[768]{0:T(1024)}, f32[768]{0:T(1024)S(1)}, u32[]{:S(2)}) copy-start(f32[768]{0:T(1024)S(1)} %convert_element_type.182) | copy-start | bytes 9220
  62.5 438.7 %copy-start.52 = (f32[768]{0:T(1024)}, f32[768]{0:T(1024)S(1)}, u32[]{:S(2)}) copy-start(f32[768]{0:T(1024)S(1)} %convert_element_type.196) | copy-start | bytes 9220
  62.6 365.0 %copy-start.61 = (f32[768]{0:T(1024)}, f32[768]{0:T(1024)S(1)}, u32[]{:S(2)}) copy-start(f32[768]{0:T(1024)S(1)} %convert_element_type.197) | copy-start | bytes 9220
  65.0 332.5 %copy-start.18 = (pred[14,12,512]{2,1,0:T(8,128)(4,1)}, pred[14,12,512]{2,1,0:T(8,128)(4,1)S(1)}, u32[]{:S(2)}) copy-start(pred[14,12,512]{2,1,0:T(8,128)(4,1)S(1)} %copy.93) | copy-start | bytes 258052
  65.8 356.3 %copy-start.1 = (bf16[1024,768]{0,1:T(8,128)(2,1)}, bf16[1024,768]{0,1:T(8,128)(2,1)S(1)}, u32[]{:S(2)}) copy-start(bf16[1024,768]{0,1:T(8,128)(2,1)S(1)} %copy.86) | copy-start | bytes 4718596
  65.8 2.0 copy-start.29
  66.1 113.0 %copy-start.40 = (f32[1024]{0:T(1024)}, f32[1024]{0:T(1024)S(1)}, u32[]{:S(2)}) copy-start(f32[1024]{0:T(1024)S(1)} %broadcast_multiply_fusion.3) | copy-start | bytes 12292
  67.8 111.3 %copy-start.46 = (f32[1024]{0:T(1024)}, f32[1024]{0:T(1024)S(1)}, u32[]{:S(2)}) copy-start(f32[1024]{0:T(1024)S(1)} %fusion.51) | copy-start | bytes 12292
  126.2 61.5 %copy-start.11 = (bf16[1024,768]{0,1:T(8,128)(2,1)}, bf16[1024,768]{0,1:T(8,128)(2,1)S(1)}, u32[]{:S(2)}) copy-start(bf16[1024,768]{0,1:T(8,128)(2,1)S(1)} %convolution_convert_fusion.1) | copy-start | bytes 4718596
  189.7 2.7 copy-start
  189.7 2.7 copy-start.16
  194.3 227.8 %copy-start.69 = (bf16[12,64,128]{2,1,0:T(8,128)(2,1)}, bf16[12,64,128]{2,1,0:T(8,128)(2,1)S(1)}, u32[]{:S(2)}) copy-start(bf16[12,64,128]{2,1,0:T(8,128)(2,1)S(1)} %convolution_convert_fusion.3) | copy-start | bytes 589828
  397.4 14.6 %copy-start.20 = (f32[14,12,64]{2,1,0:T(8,128)}, f32[14,12,64]{2,1,0:T(8,128)S(1)}, u32[]{:S(2)}) copy-start(f32[14,12,64]{2,1,0:T(8,128)S(1)} %log_add_fusion) | copy-start | bytes 129028
  422.0 3.4 copy-start.35
  425.5 75.7 %copy-start.44 = (f32[1024]{0:T(1024)}, f32[1024]{0:T(1024)S(1)}, u32[]{:S(2)}) copy-start(f32[1024]{0:T(1024)S(1)} %broadcast_multiply_fusion.2) | copy-start | bytes 12292
  427.5 73.7 %copy-start.54 = (f32[1024]{0:T(1024)}, f32[1024]{0:T(1024)S(1)}, u32[]{:S(2)}) copy-start(f32[1024]{0:T(1024)S(1)} %fusion.52) | copy-start | bytes 12292
  427.6 38.3 %copy-start.30 = (bf16[1024,768]{1,0:T(8,128)(2,1)S(1)}, bf16[1024,768]{1,0:T(8,128)(2,1)}, u32[]{:S(2)}) copy-start(bf16[1024,768]{1,0:T(8,128)(2,1)} %param.22) | copy-start | bytes 4718596
  494.0 3.7 copy-start.6
  497.7 3.5 copy-start.8
  504.6 2.8 copy-start.68
  509.7 3.7 copy-start.19
  509.7 3.7 copy-start.21
  509.7 367.5 %reduce-scatter.7.cloned.1.call-start = ((), (), s32[]{:S(2)}) async-start(), calls=%async_computation.12 | async-start | bytes 2433024 | tf_op jit(solution)/shard_map/reduce_scatter | solution.py:463
  513.4 44.0 %slice-start = ((s8[11010048]{0:T(1024)(128)(4,1)}), s8[2621440]{0:T(1024)(128)(4,1)S(1)}, s32[]{:S(2)}) async-start(s8[11010048]{0:T(1024)(128)(4,1)} %bitcast.133), calls=%async_computation.18 | async-start | bytes 5242880
  513.4 44.0 %slice-start.1 = ((s8[11010048]{0:T(1024)(128)(4,1)}), s8[4194304]{0:T(1024)(128)(4,1)S(1)}, s32[]{:S(2)}) async-start(s8[11010048]{0:T(1024)(128)(4,1)} %bitcast.133), calls=%async_computation.19 | async-start | bytes 8388608
  538.1 19.3 %slice-start.2 = ((s8[11010048]{0:T(1024)(128)(4,1)}), s8[4194304]{0:T(1024)(128)(4,1)S(1)}, s32[]{:S(2)}) async-start(s8[11010048]{0:T(1024)(128)(4,1)} %bitcast.133), calls=%async_computation.20 | async-start | bytes 8388608
  568.7 4.6 copy-start.17
  568.7 4.6 copy-start.24
  568.7 4.6 copy-start.39
  568.7 4.6 copy-start.57
  573.2 10.1 copy-start.14
  573.2 4.8 slice-start.3
  573.3 5.3 slice-start.4
  578.6 3.5 copy-start.12
  587.1 290.2 %reduce-scatter.9.cloned.1.call-start = ((), (), s32[]{:S(2)}) async-start(), calls=%async_computation.13 | async-start | bytes 2433024 | tf_op jit(solution)/shard_map/reduce_scatter | solution.py:463
  602.6 32.5 %copy-start.23 = (s32[14,12,8]{2,1,0:T(8,128)S(1)}, s32[14,12,8]{2,1,0:T(8,128)}, u32[]{:S(2)}) copy-start(s32[14,12,8]{2,1,0:T(8,128)} %copy-done.22) | copy-start | bytes 16132
  668.3 6.4 copy-start.25
  682.3 239.9 %reduce-scatter.11.cloned.1.call-start = ((), (), s32[]{:S(2)}) async-start(), calls=%async_computation.14 | async-start | bytes 2433024 | tf_op jit(solution)/shard_map/reduce_scatter | solution.py:463
  776.5 3.1 copy-start.45
  776.5 3.1 copy-start.53
  776.5 3.2 copy-start.55
  776.5 3.2 copy-start.62
  779.6 284.4 %reduce-scatter.15.cloned.1.call-start = ((), (), s32[]{:S(2)}) async-start(), calls=%async_computation.16 | async-start | bytes 9732096 | tf_op jit(solution)/shard_map/reduce_scatter | solution.py:463
  790.3 415.2 %reduce-scatter.17.cloned.1.call-start = ((), (), s32[]{:S(2)}) async-start(), calls=%async_computation.17 | async-start | bytes 9732096 | tf_op jit(solution)/shard_map/reduce_scatter | solution.py:463
  812.8 2.8 copy-start.15
  812.8 2.8 copy-start.27
  815.8 3.3 copy-start.34
  815.9 3.3 copy-start.67
  822.5 2.4 copy-start.10
  822.5 2.3 copy-start.49
  824.8 3.3 copy-start.58
  824.8 3.3 copy-start.59
  824.9 3.3 copy-start.60
  824.9 3.3 copy-start.65
  (24 other events, 36.3 us)
Sparse Core Ops, SparseCore 0:
  10.9 56.7 all-gather.8
  70.5 52.7 all-gather.10
  126.2 52.7 all-gather.6
  181.8 52.7 all-gather.12
  237.3 62.4 all-gather.14
  302.6 61.8 all-gather.16
  509.8 98.8 reduce-scatter.12
  614.6 98.6 reduce-scatter.6
  719.2 98.5 reduce-scatter.8
  823.5 98.6 reduce-scatter.10
  928.7 135.2 reduce-scatter.14
  1070.3 135.1 reduce-scatter.16
where the time goes:
time: 1220 us; the launch traced here: 1210 us
  waiting for transfers between devices  429 us (35%)
  matrix products  326 us (27%)
  local copies, waits for them, and re-layouts  313 us (26%)
  blocking collectives  83.3 us (7%)
  other arithmetic  45 us (4%)
  between operations  16.1 us (1%)
    reduce_scatter x6, waiting for transfers between devices, body(): lax.psum_scatter(totals, ('dp', 'fsdp'), scatter_dimension=0, tiled=True)  328 us
    unnamed x2, blocking collectives  83.3 us
    dot_general x6, matrix products, matmul(): return jnp.dot(left, right, preferred_element_type=f_type)  61.4 us
    all_gather x1, waiting for transfers between devices, body(): lax.all_gather(shards[5], ('dp', 'fsdp'), axis=0, tiled=True)  50 us
    all_gather x1, waiting for transfers between devices, body(): lax.all_gather(shards[4], ('dp', 'fsdp'), axis=0, tiled=True)  46.8 us
    convert_element_type x1, local copies, waits for them, and re-layouts, pick_blocks(): picked_values = jnp.einsum('bhjn,nkhd->bhjkd', onehot, value_blocks, pref...  38.9 us
    convert_element_type x1, local copies, waits for them, and re-layouts, pick_blocks(): picked_keys = jnp.einsum('bhjn,nkhd->bhjkd', onehot, key_blocks, preferre...  38.8 us
    unnamed x183, local copies, waits for them, and re-layouts  36.1 us
  transfers between devices with their start and end apart: 12, of which 5 were waited for; matrix products, arithmetic and copies ran while one was open for 52% of the time, Pallas kernels for 0%

commit v1 on v0

v1 whole, which is shorter than its diff:
```python
import functools

import jax
import jax.numpy as jnp
from jax import lax
from jax.experimental import pallas as pl
from jax.experimental.pallas import tpu as pltpu
from jax.sharding import PartitionSpec as P

H = 12
HD = 64
BLK = 64
NBLK = 16
D = H * HD
QUAD = 4 * HD
NQUAD = H // 4
PICKED = 8 * BLK
FIXED = 5 * BLK

masked_fill = -1e30
bf_type = jnp.bfloat16
f_type = jnp.float32
AXES = ("dp", "fsdp")
VMEM_LIMIT = 63 * 1024 * 1024


def dot_nn(left, right):
    return lax.dot_general(left, right, (((1,), (0,)), ((), ())), preferred_element_type=f_type)


def dot_nt(left, right):
    return lax.dot_general(left, right, (((1,), (1,)), ((), ())), preferred_element_type=f_type)


def dot_tn(left, right):
    return lax.dot_general(left, right, (((0,), (0,)), ((), ())), preferred_element_type=f_type)


def norm_parts(values):
    centre = jnp.mean(values, axis=-1, keepdims=True)
    centred = values - centre
    inverse = lax.rsqrt(jnp.mean(centred * centred, axis=-1, keepdims=True) + 1e-05)
    return centred * inverse, inverse


def norm_back(upstream, gain, unit, inverse):
    scaled = upstream * gain
    first = jnp.mean(scaled, axis=-1, keepdims=True)
    second = jnp.mean(scaled * unit, axis=-1, keepdims=True)
    return inverse * (scaled - first - unit * second)


def lane_heads(width):
    return lax.broadcasted_iota(jnp.int32, (1, width), 1) // HD


def spread_heads(rows):
    heads = lane_heads(QUAD)
    zero = jnp.zeros_like(rows)
    return jnp.concatenate([jnp.where(heads == item, rows, zero) for item in range(4)], axis=0)


def fold_heads(stacked):
    heads = lane_heads(QUAD)
    total = None
    for item in range(4):
        piece = jnp.where(heads == item, stacked[item * BLK : (item + 1) * BLK], 0.0)
        total = piece if total is None else total + piece
    return total


def pick_random(rand_ref, source, target, block, quad):
    upper = lax.broadcasted_iota(jnp.int32, (1, 2 * HD), 1) >= HD
    for slot in range(3):
        for pair in range(2):
            head = quad * 4 + pair * 2
            lanes = pl.ds(quad * QUAD + pair * 2 * HD, 2 * HD)
            first = rand_ref[((block - 2) * H + head) * 3 + slot]
            second = rand_ref[((block - 2) * H + head + 1) * 3 + slot]
            left = source[pl.ds(pl.multiple_of(first * BLK, BLK), BLK), lanes]
            right = source[pl.ds(pl.multiple_of(second * BLK, BLK), BLK), lanes]
            target[FIXED + slot * BLK : FIXED + (slot + 1) * BLK, pair * 2 * HD : (pair + 1) * 2 * HD] = jnp.where(
                upper, right, left
            )


def front_kernel(
    rand_ref,
    x_ref,
    lane_bias_ref,
    global_bias_ref,
    gain_ref,
    shift_ref,
    query_bias_ref,
    value_bias_ref,
    out_bias_ref,
    query_weight_ref,
    key_weight_ref,
    value_weight_ref,
    out_weight_ref,
    normed_ref,
    query_ref,
    key_ref,
    value_ref,
    mixed_ref,
    residual_ref,
    picked_key,
    picked_value,
):
    slots = x_ref.shape[0]
    step = 256

    @pl.loop(0, slots // step)
    def _(turn):
        rows = pl.ds(pl.multiple_of(turn * step, step), step)
        unit, inverse = norm_parts(x_ref[rows, :].astype(f_type))
        normed = (unit * gain_ref[...] + shift_ref[...]).astype(bf_type)
        normed_ref[rows, :] = normed
        query_ref[rows, :] = (
            (dot_nn(normed, query_weight_ref[...]) + query_bias_ref[...]) * 0.125
        ).astype(bf_type)
        key_ref[rows, :] = dot_nn(normed, key_weight_ref[...]).astype(bf_type)
        value_ref[rows, :] = (dot_nn(normed, value_weight_ref[...]) + value_bias_ref[...]).astype(bf_type)

    key_ref[pl.ds(slots, BLK), :] = jnp.zeros((BLK, D), bf_type)
    value_ref[pl.ds(slots, BLK), :] = jnp.zeros((BLK, D), bf_type)

    for quad in range(NQUAD):
        lanes = pl.ds(quad * QUAD, QUAD)

        @pl.loop(0, 2)
        def _(block):
            rows = pl.ds(pl.multiple_of(block * BLK, BLK), BLK)
            query = spread_heads(query_ref[rows, lanes])
            scores = dot_nt(query, key_ref[pl.ds(0, slots), lanes]) + global_bias_ref[...]
            top = jnp.max(scores, axis=-1, keepdims=True)
            powers = jnp.exp(scores - top)
            total = jnp.sum(powers, axis=-1, keepdims=True)
            out = dot_nn(powers.astype(bf_type), value_ref[pl.ds(0, slots), lanes]) / total
            mixed_ref[rows, lanes] = fold_heads(out).astype(bf_type)

        picked_key[0 : 2 * BLK, :] = key_ref[0 : 2 * BLK, lanes]
        picked_value[0 : 2 * BLK, :] = value_ref[0 : 2 * BLK, lanes]

        @pl.loop(2, NBLK)
        def _(block):
            rows = pl.ds(pl.multiple_of(block * BLK, BLK), BLK)
            near = pl.ds(pl.multiple_of((block - 1) * BLK, BLK), 3 * BLK)
            picked_key[2 * BLK : FIXED, :] = key_ref[near, lanes]
            picked_value[2 * BLK : FIXED, :] = value_ref[near, lanes]
            pick_random(rand_ref, key_ref, picked_key, block, quad)
            pick_random(rand_ref, value_ref, picked_value, block, quad)
            query = spread_heads(query_ref[rows, lanes])
            scores = dot_nt(query, picked_key[...])
            bias = lane_bias_ref[(block - 2) * NQUAD + quad]
            scores = jnp.concatenate(
                [scores[item * BLK : (item + 1) * BLK] + bias[item : item + 1] for item in range(4)], axis=0
            )
            top = jnp.max(scores, axis=-1, keepdims=True)
            powers = jnp.exp(scores - top)
            total = jnp.sum(powers, axis=-1, keepdims=True)
            out = dot_nn(powers.astype(bf_type), picked_value[...]) / total
            mixed_ref[rows, lanes] = fold_heads(out).astype(bf_type)

    @pl.loop(0, slots // step)
    def _(turn):
        rows = pl.ds(pl.multiple_of(turn * step, step), step)
        residual_ref[rows, :] = (
            x_ref[rows, :].astype(f_type) + dot_nn(mixed_ref[rows, :], out_weight_ref[...]) + out_bias_ref[...]
        )


ROOT_HALF = 0.7071067811865476
DENSITY = 0.3989422804014327


def feed_kernel(
    residual_ref,
    cot_ref,
    mixed_ref,
    gain_ref,
    shift_ref,
    up_bias_ref,
    down_bias_ref,
    up_weight_ref,
    down_weight_ref,
    out_weight_ref,
    layer_ref,
    up_grad_ref,
    down_grad_ref,
    out_grad_ref,
    grad_resid_ref,
    grad_mixed_ref,
    small_ref,
    up_bias_grad_ref,
    act_ref,
    grad_hidden_ref,
    normed_ref,
    grad_attn_ref,
    branch_acc,
    back_acc,
):
    slots = residual_ref.shape[0]
    hidden_width = up_weight_ref.shape[1]
    step = 256
    part = 512

    small_ref[...] = jnp.zeros(small_ref.shape, f_type)
    up_bias_grad_ref[...] = jnp.zeros(up_bias_grad_ref.shape, f_type)

    @pl.loop(0, slots // step)
    def _(turn):
        rows = pl.ds(pl.multiple_of(turn * step, step), step)
        unit, inverse = norm_parts(residual_ref[rows, :])
        normed = (unit * gain_ref[...] + shift_ref[...]).astype(bf_type)
        normed_ref[rows, :] = normed
        cot = cot_ref[rows, :]
        branch_acc[...] = jnp.zeros(branch_acc.shape, f_type)
        back_acc[...] = jnp.zeros(back_acc.shape, f_type)

        @pl.loop(0, hidden_width // part)
        def _(piece):
            lanes = pl.ds(pl.multiple_of(piece * part, part), part)
            hidden = dot_nn(normed_ref[rows, :], up_weight_ref[:, lanes]) + up_bias_ref[:, lanes]
            cumulative = 0.5 * (1.0 + lax.erf(hidden * ROOT_HALF))
            act = (hidden * cumulative).astype(bf_type)
            act_ref[rows, lanes] = act
            slope = cumulative + hidden * (DENSITY * jnp.exp(-0.5 * hidden * hidden))
            down = down_weight_ref[lanes, :]
            branch_acc[...] += dot_nn(act, down)
            grad_hidden = (dot_nt(cot_ref[rows, :], down) * slope).astype(bf_type)
            grad_hidden_ref[rows, lanes] = grad_hidden
            up_bias_grad_ref[:, lanes] += jnp.sum(grad_hidden.astype(f_type), axis=0, keepdims=True)
            back_acc[...] += dot_nt(grad_hidden, up_weight_ref[:, lanes])

        layer_ref[rows, :] = (residual_ref[rows, :] + branch_acc[...] + down_bias_ref[...]).astype(bf_type)
        unit, inverse = norm_parts(residual_ref[rows, :])
        upstream = back_acc[...]
        wide_cot = cot.astype(f_type)
        grad_resid = wide_cot + norm_back(upstream, gain_ref[...], unit, inverse)
        grad_resid_ref[rows, :] = grad_resid
        grad_attn = grad_resid.astype(bf_type)
        grad_attn_ref[rows, :] = grad_attn
        grad_mixed_ref[rows, :] = dot_nt(grad_attn, out_weight_ref[...]).astype(bf_type)
        small_ref[0:1, :] += jnp.sum(upstream * unit, axis=0, keepdims=True)
        small_ref[1:2, :] += jnp.sum(upstream, axis=0, keepdims=True)
        small_ref[2:3, :] += jnp.sum(wide_cot, axis=0, keepdims=True)
        small_ref[3:4, :] += jnp.sum(grad_attn.astype(f_type), axis=0, keepdims=True)

    tile = 256

    @pl.loop(0, hidden_width // tile)
    def _(piece):
        lanes = pl.ds(pl.multiple_of(piece * tile, tile), tile)
        down_grad_ref[lanes, :] = dot_tn(act_ref[:, lanes], cot_ref[...]).astype(bf_type)

    @pl.loop(0, D // tile)
    def _(piece):
        lanes = pl.ds(pl.multiple_of(piece * tile, tile), tile)
        up_grad_ref[lanes, :] = dot_tn(normed_ref[:, lanes], grad_hidden_ref[...]).astype(bf_type)
        out_grad_ref[lanes, :] = dot_tn(mixed_ref[:, lanes], grad_attn_ref[...]).astype(bf_type)


def soft_back(scores_t, prob_grad_t):
    top = jnp.max(scores_t, axis=0, keepdims=True)
    powers = jnp.exp(scores_t - top)
    inverse = 1.0 / jnp.sum(powers, axis=0, keepdims=True)
    probs = powers * inverse
    delta = jnp.sum(probs * prob_grad_t, axis=0, keepdims=True)
    return probs.astype(bf_type), (probs * (prob_grad_t - delta)).astype(bf_type)


def back_kernel(
    rand_ref,
    length_ref,
    limit_ref,
    query_ref,
    key_ref,
    value_ref,
    grad_mixed_ref,
    normed_ref,
    x_ref,
    grad_resid_ref,
    gain_ref,
    query_weight_ref,
    key_weight_ref,
    value_weight_ref,
    input_grad_ref,
    query_grad_ref,
    key_grad_ref,
    value_grad_ref,
    small_ref,
    picked_key,
    picked_value,
    key_acc,
    value_acc,
    grad_query_ref,
    grad_key_ref,
    grad_value_ref,
):
    slots = x_ref.shape[0]
    key_acc[...] = jnp.zeros(key_acc.shape, f_type)
    value_acc[...] = jnp.zeros(value_acc.shape, f_type)
    small_ref[...] = jnp.zeros(small_ref.shape, f_type)
    length = length_ref[0]
    upper = lax.broadcasted_iota(jnp.int32, (1, 2 * HD), 1) >= HD

    for quad in range(NQUAD):
        lanes = pl.ds(quad * QUAD, QUAD)

        @pl.loop(0, 2)
        def _(block):
            rows = pl.ds(pl.multiple_of(block * BLK, BLK), BLK)
            query = spread_heads(query_ref[rows, lanes])
            grad = spread_heads(grad_mixed_ref[rows, lanes])
            keys = key_ref[pl.ds(0, slots), lanes]
            scores_t = dot_nt(keys, query)
            scores_t = jnp.where(
                lax.broadcasted_iota(jnp.int32, scores_t.shape, 0) < length, scores_t, masked_fill
            )
            prob_grad_t = dot_nt(value_ref[pl.ds(0, slots), lanes], grad)
            probs, dscore = soft_back(scores_t, prob_grad_t)
            key_acc[pl.ds(0, slots), lanes] += dot_nn(dscore, query)
            value_acc[pl.ds(0, slots), lanes] += dot_nn(probs, grad)
            grad_query_ref[rows, lanes] = fold_heads(dot_tn(dscore, keys)).astype(bf_type)

        picked_key[0 : 2 * BLK, :] = key_ref[0 : 2 * BLK, lanes]
        picked_value[0 : 2 * BLK, :] = value_ref[0 : 2 * BLK, lanes]

        @pl.loop(2, NBLK)
        def _(block):
            rows = pl.ds(pl.multiple_of(block * BLK, BLK), BLK)
            near = pl.ds(pl.multiple_of((block - 1) * BLK, BLK), 3 * BLK)
            picked_key[2 * BLK : FIXED, :] = key_ref[near, lanes]
            picked_value[2 * BLK : FIXED, :] = value_ref[near, lanes]
            pick_random(rand_ref, key_ref, picked_key, block, quad)
            pick_random(rand_ref, value_ref, picked_value, block, quad)
            query = spread_heads(query_ref[rows, lanes])
            grad = spread_heads(grad_mixed_ref[rows, lanes])
            scores_t = dot_nt(picked_key[...], query)
            limits = limit_ref[block - 2, :, lanes]
            place = lax.broadcasted_iota(jnp.int32, (BLK, QUAD), 0)
            scores_t = jnp.concatenate(
                [scores_t[0 : 2 * BLK]]
                + [
                    jnp.where(
                        place < limits[item : item + 1], scores_t[item * BLK : (item + 1) * BLK], masked_fill
                    )
                    for item in range(2, 8)
                ],
                axis=0,
            )
            prob_grad_t = dot_nt(picked_value[...], grad)
            probs, dscore = soft_back(scores_t, prob_grad_t)
            grad_query_ref[rows, lanes] = fold_heads(dot_tn(dscore, picked_key[...])).astype(bf_type)
            for acc, piece in ((key_acc, dot_nn(dscore, query)), (value_acc, dot_nn(probs, grad))):
                acc[pl.ds(0, 2 * BLK), lanes] += piece[0 : 2 * BLK]
                acc[near, lanes] += piece[2 * BLK : FIXED]
                for slot in range(3):
                    for pair in range(2):
                        head = quad * 4 + pair * 2
                        pair_lanes = pl.ds(quad * QUAD + pair * 2 * HD, 2 * HD)
                        part = piece[
                            FIXED + slot * BLK : FIXED + (slot + 1) * BLK, pair * 2 * HD : (pair + 1) * 2 * HD
                        ]
                        first = rand_ref[((block - 2) * H + head) * 3 + slot]
                        second = rand_ref[((block - 2) * H + head + 1) * 3 + slot]
                        acc[pl.ds(pl.multiple_of(first * BLK, BLK), BLK), pair_lanes] += jnp.where(
                            upper, 0.0, part
                        )
                        acc[pl.ds(pl.multiple_of(second * BLK, BLK), BLK), pair_lanes] += jnp.where(
                            upper, part, 0.0
                        )

    step = 256

    @pl.loop(0, slots // step)
    def _(turn):
        rows = pl.ds(pl.multiple_of(turn * step, step), step)
        grad_query = grad_query_ref[rows, :]
        grad_key = key_acc[rows, :].astype(bf_type)
        grad_value = value_acc[rows, :].astype(bf_type)
        grad_key_ref[rows, :] = grad_key
        grad_value_ref[rows, :] = grad_value
        upstream = (
            dot_nt(grad_query, query_weight_ref[...]) * 0.125
            + dot_nt(grad_key, key_weight_ref[...])
            + dot_nt(grad_value, value_weight_ref[...])
        )
        unit, inverse = norm_parts(x_ref[rows, :].astype(f_type))
        input_grad_ref[rows, :] = grad_resid_ref[rows, :] + norm_back(upstream, gain_ref[...], unit, inverse)
        small_ref[0:1, :] += jnp.sum(upstream * unit, axis=0, keepdims=True)
        small_ref[1:2, :] += jnp.sum(upstream, axis=0, keepdims=True)
        small_ref[2:3, :] += jnp.sum(grad_query.astype(f_type), axis=0, keepdims=True) * 0.125
        small_ref[3:4, :] += jnp.sum(grad_value.astype(f_type), axis=0, keepdims=True)

    tile = 256

    @pl.loop(0, D // tile)
    def _(piece):
        lanes = pl.ds(pl.multiple_of(piece * tile, tile), tile)
        normed = normed_ref[:, lanes]
        query_grad_ref[lanes, :] = (dot_tn(normed, grad_query_ref[...]) * 0.125).astype(bf_type)
        key_grad_ref[lanes, :] = dot_tn(normed, grad_key_ref[...]).astype(bf_type)
        value_grad_ref[lanes, :] = dot_tn(normed, grad_value_ref[...]).astype(bf_type)


def shape(dims, kind):
    return jax.ShapeDtypeStruct(dims, kind)


def in_vmem(count):
    return [pl.BlockSpec(memory_space=pltpu.VMEM)] * count


def in_smem(count):
    return [pl.BlockSpec(memory_space=pltpu.SMEM)] * count


def masks(length, rand_rows):
    later = jnp.arange(2, NBLK, dtype=jnp.int32)
    fixed = jnp.stack([jnp.zeros_like(later), jnp.ones_like(later), later - 1, later, later + 1], axis=-1)
    fixed = jnp.broadcast_to(fixed[:, None, :], (NBLK - 2, H, 5))
    chosen = jnp.concatenate([fixed, rand_rows], axis=-1)
    limits = length - chosen * BLK
    limits = jnp.where(chosen >= NBLK, 0, limits)
    live = jnp.arange(BLK, dtype=jnp.int32) < limits[..., None]
    lane_bias = jnp.where(live, 0.0, masked_fill).astype(f_type).reshape((NBLK - 2) * NQUAD, 4, PICKED)
    limit_rows = jnp.repeat(limits.transpose(0, 2, 1), HD, axis=2)
    global_bias = jnp.where(jnp.arange(NBLK * BLK) < length, 0.0, masked_fill).astype(f_type)[None]
    return lane_bias, global_bias, limit_rows


def front_call(rand_flat, window, lane_bias, global_bias, vectors, weights):
    slots = window.shape[0]
    return pl.pallas_call(
        front_kernel,
        out_shape=(
            shape((slots, D), bf_type),
            shape((slots, D), bf_type),
            shape((slots + BLK, D), bf_type),
            shape((slots + BLK, D), bf_type),
            shape((slots, D), bf_type),
            shape((slots, D), f_type),
        ),
        in_specs=in_smem(1) + in_vmem(12),
        out_specs=tuple(in_vmem(6)),
        scratch_shapes=[pltpu.VMEM((PICKED, QUAD), bf_type)] * 2,
        compiler_params=pltpu.CompilerParams(vmem_limit_bytes=VMEM_LIMIT),
        name="front",
    )(rand_flat, window, lane_bias, global_bias, *vectors, *weights)


def feed_call(residual, cotangent, mixed, vectors, weights):
    slots = residual.shape[0]
    width = weights[0].shape[1]
    return pl.pallas_call(
        feed_kernel,
        out_shape=(
            shape((slots, D), bf_type),
            shape((D, width), bf_type),
            shape((width, D), bf_type),
            shape((D, D), bf_type),
            shape((slots, D), f_type),
            shape((slots, D), bf_type),
            shape((8, D), f_type),
            shape((1, width), f_type),
        ),
        in_specs=in_vmem(10),
        out_specs=tuple(in_vmem(8)),
        scratch_shapes=[
            pltpu.VMEM((slots, width), bf_type),
            pltpu.VMEM((slots, width), bf_type),
            pltpu.VMEM((slots, D), bf_type),
            pltpu.VMEM((slots, D), bf_type),
            pltpu.VMEM((256, D), f_type),
            pltpu.VMEM((256, D), f_type),
        ],
        compiler_params=pltpu.CompilerParams(vmem_limit_bytes=VMEM_LIMIT),
        name="feed",
    )(residual, cotangent, mixed, *vectors, *weights)


def back_call(rand_flat, length, limits, query, key, value, grad_mixed, normed, window, grad_resid, gain, weights):
    slots = window.shape[0]
    return pl.pallas_call(
        back_kernel,
        out_shape=(
            shape((slots, D), f_type),
            shape((D, D), bf_type),
            shape((D, D), bf_type),
            shape((D, D), bf_type),
            shape((8, D), f_type),
        ),
        in_specs=in_smem(2) + in_vmem(12),
        out_specs=tuple(in_vmem(5)),
        scratch_shapes=[
            pltpu.VMEM((PICKED, QUAD), bf_type),
            pltpu.VMEM((PICKED, QUAD), bf_type),
            pltpu.VMEM((slots + BLK, D), f_type),
            pltpu.VMEM((slots + BLK, D), f_type),
            pltpu.VMEM((slots, D), bf_type),
            pltpu.VMEM((slots, D), bf_type),
            pltpu.VMEM((slots, D), bf_type),
        ],
        compiler_params=pltpu.CompilerParams(vmem_limit_bytes=VMEM_LIMIT),
        name="back",
    )(rand_flat, length, limits, query, key, value, grad_mixed, normed, window, grad_resid, gain, *weights)


def window_pass(window, length, rand_rows, cotangent, params):
    (
        first_gain,
        first_shift,
        query_weight,
        query_bias,
        key_weight,
        value_weight,
        value_bias,
        out_weight,
        out_bias,
        second_gain,
        second_shift,
        up_weight,
        up_bias,
        down_weight,
        down_bias,
    ) = params
    lane_bias, global_bias, limits = masks(length[0], rand_rows)
    rand_flat = rand_rows.reshape(-1)
    normed, query, key, value, mixed, residual = front_call(
        rand_flat,
        window,
        lane_bias,
        global_bias,
        (first_gain, first_shift, query_bias, value_bias, out_bias),
        (query_weight, key_weight, value_weight, out_weight),
    )
    layer_out, up_grad, down_grad, out_grad, grad_resid, grad_mixed, feed_small, up_bias_grad = feed_call(
        residual,
        cotangent,
        mixed,
        (second_gain, second_shift, up_bias, down_bias),
        (up_weight, down_weight, out_weight),
    )
    input_grad, query_grad, key_grad, value_grad, back_small = back_call(
        rand_flat,
        length,
        limits,
        query,
        key,
        value,
        grad_mixed,
        normed,
        window,
        grad_resid,
        first_gain,
        (query_weight, key_weight, value_weight),
    )
    grads = (
        back_small[0],
        back_small[1],
        query_grad,
        back_small[2],
        key_grad,
        value_grad,
        back_small[3],
        out_grad,
        feed_small[3],
        feed_small[0],
        feed_small[1],
        up_grad,
        up_bias_grad[0],
        down_grad,
        feed_small[2],
    )
    return layer_out, input_grad, grads


NARROW = (0, 1, 3, 6, 8, 9, 10, 14)


def body(tokens, lengths, rand_blocks, cotangent, *shards):
    rows = shards[0].shape[0]
    narrow = jnp.stack([shards[item] for item in NARROW], axis=1)
    wide_bias = shards[12].reshape(rows, -1)
    spare = jnp.zeros((rows, 128 - len(NARROW) - wide_bias.shape[1]), bf_type)
    first = jnp.concatenate([shards[2], shards[4], shards[5], shards[7], narrow, wide_bias, spare], axis=1)
    gathered = lax.all_gather(first, AXES, axis=0, tiled=True)
    up_weight = lax.all_gather(shards[11], AXES, axis=0, tiled=True)
    down_weight = lax.all_gather(shards[13], AXES, axis=0, tiled=True)
    query_weight, key_weight, value_weight, out_weight = (gathered[:, D * item : D * (item + 1)] for item in range(4))
    tail = gathered[:, 4 * D :].astype(f_type)
    whole = [None] * 15
    for place, item in enumerate(NARROW):
        whole[item] = tail[:, place][None]
    whole[12] = tail[:, len(NARROW) : len(NARROW) + wide_bias.shape[1]].reshape(1, -1)
    whole[2], whole[4], whole[5], whole[7] = query_weight, key_weight, value_weight, out_weight
    whole[11], whole[13] = up_weight, down_weight

    windows = lengths.shape[0]
    slots = tokens.shape[0] // windows
    layers, inputs, totals = [], [], None
    for item in range(windows):
        part = slice(item * slots, (item + 1) * slots)
        layer_out, input_grad, grads = window_pass(
            tokens[part], lengths[item : item + 1], rand_blocks[item], cotangent[part], whole
        )
        layers.append(layer_out)
        inputs.append(input_grad)
        totals = grads if totals is None else tuple(a + b for a, b in zip(totals, grads))
    layer_out = layers[0] if windows == 1 else jnp.concatenate(layers)
    input_grad = inputs[0] if windows == 1 else jnp.concatenate(inputs)

    def scatter(values):
        return lax.psum_scatter(values.astype(bf_type), AXES, scatter_dimension=0, tiled=True).astype(f_type)

    owned_down = scatter(totals[13])
    owned_up = scatter(totals[11])
    narrow_grads = jnp.stack([totals[item] for item in NARROW], axis=1)
    wide_grads = totals[12].reshape(D, -1)
    spare = jnp.zeros((D, 128 - len(NARROW) - wide_grads.shape[1]), f_type)
    small = jnp.concatenate([narrow_grads, wide_grads, spare], axis=1).astype(bf_type)
    owned = scatter(jnp.concatenate([totals[2], totals[4], totals[5], totals[7], small], axis=1))
    result = [None] * 15
    for place, item in enumerate((2, 4, 5, 7)):
        result[item] = owned[:, D * place : D * (place + 1)]
    for place, item in enumerate(NARROW):
        result[item] = owned[:, 4 * D + place]
    start = 4 * D + len(NARROW)
    result[12] = owned[:, start : start + wide_bias.shape[1]].reshape(-1)
    result[11], result[13] = owned_up, owned_down
    return (layer_out, input_grad, *result)


def solution(mesh):
    row = P(AXES, None)
    flat = P(AXES)
    params = (flat, flat, row, flat, row, row, flat, row, flat, flat, flat, row, flat, row, flat)
    in_specs = (row, flat, P(AXES, None, None, None), row) + params
    out_specs = (row, row) + params
    return jax.shard_map(body, mesh=mesh, in_specs=in_specs, out_specs=out_specs, check_vma=False)
```

time: 1220 us -> 610 us (0.50)
  matrix products: 326 us -> 0 us
  local copies, waits for them, and re-layouts: 313 us -> 39.8 us
  Pallas kernels: 0 us -> 175 us
  blocking collectives: 83.3 us -> 0 us
  waiting for transfers between devices: 429 us -> 372 us
  other arithmetic: 45 us -> 7.5 us
    dot_general x34 -> x0, matrix products: 326 us -> none  [the longest x6 61.4 us: matmul(): return jnp.dot(left, right, preferred_element_type=f_type)]
    reduce_scatter x6 -> x2, waiting for transfers between devices: 328 us -> 134 us  [scatter(): lax.psum_scatter(values.astype(bf_type), AXES, scatter_dimension=0, tiled...]
    pallas_call x0 -> x3, Pallas kernels: none -> 175 us  [the longest x1 68.6 us: back_call(): pl.pallas_call(back_kernel, out_shape=(shape((slots, D), f_type), shape((...]
    reshape x8 -> x4, local copies, waits for them, and re-layouts: 138 us -> 3.21 us  [the longest x1 1 us: masks(): limit_rows = jnp.repeat(limits.transpose(0, 2, 1), HD, axis=2)]
    unnamed x12 -> x7, waiting for transfers between devices: 3.74 us -> 106 us
    unnamed x2 -> x0, blocking collectives: 83.3 us -> none
    convert_element_type x2 -> x0, local copies, waits for them, and re-layouts: 77.7 us -> none  [the longest x1 38.9 us: pick_blocks(): picked_values = jnp.einsum('bhjn,nkhd->bhjkd', onehot, value_blocks, pref...]
    all_gather x6 -> x3, waiting for transfers between devices: 96.8 us -> 132 us  [the longest x1 65.2 us: body(): down_weight = lax.all_gather(shards[13], AXES, axis=0, tiled=True)]
  transfers between devices with their start and end apart: 12 -> 6, of which waited for: 5 -> 6; matrix products, arithmetic and copies ran while one was open for 52% -> 6% of each run, Pallas kernels for 0% -> 19%
where the time goes in v1:
time: 610 us
  waiting for transfers between devices  372 us (61%)
  Pallas kernels  175 us (29%)
  local copies, waits for them, and re-layouts  39.8 us (7%)
  between operations  15 us (2%)
  other arithmetic  7.5 us (1%)
    reduce_scatter x2, waiting for transfers between devices, scatter(): lax.psum_scatter(values.astype(bf_type), AXES, scatter_dimension=0, tiled...  134 us
    unnamed x7, waiting for transfers between devices  106 us
    pallas_call x1, Pallas kernels, back_call(): pl.pallas_call(back_kernel, out_shape=(shape((slots, D), f_type), shape((...  68.6 us
    all_gather x1, waiting for transfers between devices, body(): down_weight = lax.all_gather(shards[13], AXES, axis=0, tiled=True)  65.2 us
    pallas_call x1, Pallas kernels, feed_call(): pl.pallas_call(feed_kernel, out_shape=(shape((slots, D), bf_type), shape(...  61.6 us
    all_gather x1, waiting for transfers between devices, body(): gathered = lax.all_gather(first, AXES, axis=0, tiled=True)  60 us
    pallas_call x1, Pallas kernels, front_call(): pl.pallas_call(front_kernel, out_shape=(shape((slots, D), bf_type), shape...  44.8 us
  transfers between devices with their start and end apart: 6, of which 6 were waited for; matrix products, arithmetic and copies ran while one was open for 6% of the time, Pallas kernels for 19%

profile of v1, /device:TPU:0, one launch (start us, length us, event | category | flops | bytes accessed | tf_op | source)
XLA Modules:
  0.0 609.5 jit_solution(9193320139683846401)
XLA Ops:
  7.2 0.7 copy.68
  8.0 0.7 copy.69
  8.7 0.7 copy.70
  9.5 0.7 copy.71
  10.2 0.7 copy.72
  11.0 0.7 copy.73
  11.7 0.7 copy.74
  12.5 0.7 copy.75
  13.2 0.7 reshape.106
  14.0 1.6 concatenate.23
  15.6 0.7 all-gather.6.cloned.1.call-update
  16.4 0.7 all-gather.8.cloned.1.call-update
  17.1 0.8 copy.84
  18.0 0.9 copy.65
  19.6 0.1 stack.30
  19.8 0.1 copy.67
  19.9 0.2 lt.36
  20.2 0.2 lt.37
  20.5 0.8 reshape_squeeze.7.rand_ref
  21.3 0.6 compare_select_fusion.1.global_bias_ref
  21.9 0.8 compare_select_fusion.lane_bias_ref
  22.7 60.0 %all-gather.4.cloned.1.call-done = bf16[768,3200]{1,0:T(8,128)(2,1)} async-done(((bf16[24,3200]{1,0:T(8,128)(2,1)}), bf16[768,3200]{1,0:T(8,128)(2,1)}) %all-gather.4.cloned.1.call-update) | async-done | bytes 4915216 | tf_op jit(solution)/shard_map/all_gather | solution.py:589
  82.8 1.0 slice_convert_fusion
  83.7 0.2 slice.160
  83.9 1.6 slice_reduce_fusion
  85.5 0.6 broadcast_in_dim_squeeze.24.gain_ref
  86.1 0.6 broadcast_in_dim_squeeze.25.shift_ref
  86.7 0.6 broadcast_in_dim_squeeze.26.query_bias_ref
  87.2 0.6 broadcast_in_dim_squeeze.27.value_bias_ref
  87.8 0.6 broadcast_in_dim_squeeze.28.out_bias_ref
  88.4 0.6 broadcast_in_dim_squeeze.29.gain_ref
  89.0 0.6 broadcast_in_dim_squeeze.30.shift_ref
  89.6 0.6 broadcast_in_dim_squeeze.31.down_bias_ref
  90.2 0.9 reshape.107.up_bias_ref
  91.0 4.7 fusion.5
  95.7 44.8 %front.1 = (bf16[1024,768]{1,0:T(8,128)(2,1)}, bf16[1024,768]{1,0:T(8,128)(2,1)}, bf16[1088,768]{1,0:T(8,128)(2,1)}, bf16[1088,768]{1,0:T(8,128)(2,1)}, bf16[1024,768]{1,0:T(8,128)(2,1)}, /*index=5*/f32[1024,768]{1,0:T(8,128)}) custom-call(s32[504]{0:T(512)} %reshape_squeeze.7.rand_ref, bf16[1024,768]{1,0:T(8,128)(2,1)} %x_ref.3, ...), custom_call_target="tpu_custom_call" | custom-call | tf_op jit(solution)/shard_map/front/pallas_call | solution.py:436
  140.5 7.1 %all-gather.6.cloned.1.call-done.up_weight_ref = bf16[768,3072]{1,0:T(8,128)(2,1)} async-done(((bf16[24,3072]{1,0:T(8,128)(2,1)}), bf16[768,3072]{1,0:T(8,128)(2,1)}) %all-gather.6.cloned.1.call-update) | async-done | bytes 4718608 | tf_op jit(solution)/shard_map/all_gather | solution.py:590
  147.6 65.2 %all-gather.8.cloned.1.call-done.down_weight_ref = bf16[3072,768]{1,0:T(8,128)(2,1)} async-done(((bf16[96,768]{1,0:T(8,128)(2,1)}), bf16[3072,768]{1,0:T(8,128)(2,1)}) %all-gather.8.cloned.1.call-update) | async-done | bytes 4718608 | tf_op jit(solution)/shard_map/all_gather | solution.py:591
  212.8 61.6 %feed.1 = (bf16[1024,768]{1,0:T(8,128)(2,1)}, bf16[768,3072]{1,0:T(8,128)(2,1)}, bf16[3072,768]{1,0:T(8,128)(2,1)}, bf16[768,768]{1,0:T(8,128)(2,1)}, f32[1024,7...) custom-call(f32[1024,768]{1,0:T(8,128)} %get-tuple-element.36.residual_ref, ...), custom_call_target="tpu_custom_call" | custom-call | tf_op jit(solution)/shard_map/feed/pallas_call | solution.py:457
  274.5 0.5 reduce-scatter.8.cloned.1.call-update
  275.1 0.3 broadcast_in_dim.45
  275.4 1.0 reshape.108.limit_ref
  276.4 68.6 %back.1 = (f32[1024,768]{1,0:T(8,128)}, bf16[768,768]{1,0:T(8,128)(2,1)}, bf16[768,768]{1,0:T(8,128)(2,1)}, bf16[768,768]{1,0:T(8,128)(2,1)}, f32[8,768]{1,0:T(8,128)}) custom-call(s32[504]{0:T(512)} %reshape_squeeze.7.rand_ref, s32[1]{0:T(128)} %copy.85.length_ref, s32[14,8,768]{2,1,0:T(8,128)} %reshape.108.limit_ref, ...), custom_call_target="tpu_custom_call" | custom-call | tf_op jit(solution)/shard_map/back/pallas_call | solution.py:486
  345.0 0.8 convert.34
  345.9 0.2 copy.76
  346.1 0.2 copy.77
  346.2 0.2 copy.78
  346.4 0.2 copy.79
  346.7 0.2 copy.80
  346.9 0.2 copy.81
  347.1 0.2 copy.82
  347.3 0.2 copy.83
  347.5 0.4 reshape_squeeze.8
  348.0 9.1 %concatenate.24 = bf16[768,3200]{1,0:T(8,128)(2,1)} concatenate(bf16[768,768]{1,0:T(8,128)(2,1)} %get-tuple-element.46, bf16[768,768]{1,0:T(8,128)(2,1)} %get-tuple-element.47, bf16[768,768]{1,0:T(8,128)(2,1)} %get-tuple-element.48, bf16[768,768]{1,0:T(8,128)(2,1)S(1)} %copy-done, bf16[768,1]{1,0:T(8,128)(2,1)S(1)} %copy.76, bf16[768,1]{1,0:T(8,128)(2,1)S(1)} %copy.77, ...), dimensions={1} | concatenate | bytes 9830400 | tf_op jit(solution)/shard_map/concatenate | solution.py:624
  357.1 23.4 %reduce-scatter.6.cloned.1.call-done = bf16[24,3072]{1,0:T(8,128)(2,1)} async-done(((bf16[768,3072]{1,0:T(8,128)(2,1)}), bf16[24,3072]{1,0:T(8,128)(2,1)}) %reduce-scatter.6.cloned.1.call-update) | async-done | bytes 147472 | tf_op jit(solution)/shard_map/reduce_scatter | solution.py:616
  380.5 1.6 convert_element_type.15
  382.1 110.4 %reduce-scatter.8.cloned.1.call-done = bf16[96,768]{1,0:T(8,128)(2,1)} async-done(((bf16[3072,768]{1,0:T(8,128)(2,1)}), bf16[96,768]{1,0:T(8,128)(2,1)}) %reduce-scatter.8.cloned.1.call-update) | async-done | bytes 147472 | tf_op jit(solution)/shard_map/reduce_scatter | solution.py:616
  492.6 1.6 convert_element_type.16
  494.2 103.8 %reduce-scatter.10.cloned.1.call-done = bf16[24,3200]{1,0:T(8,128)(2,1)} async-done(((bf16[768,3200]{1,0:T(8,128)(2,1)}), bf16[24,3200]{1,0:T(8,128)(2,1)}) %reduce-scatter.10.cloned.1.call-update) | async-done | bytes 153616
  598.0 0.9 convert_element_type.14
  598.9 0.8 slice_reduce_fusion.8
  599.8 0.8 slice.181
  600.5 0.6 reshape.109
  601.1 1.5 fusion.6
  (29 shorter events, 0.6 us)
Async XLA Ops:
  7.2 75.6 %all-gather.4.cloned.1.call-start = ((), (), s32[]{:S(2)}) async-start(), calls=%async_computation.3 | async-start | bytes 5068800 | tf_op jit(solution)/shard_map/all_gather | solution.py:589
  15.6 132.0 %all-gather.6.cloned.1.call-start = ((), (), s32[]{:S(2)}) async-start(), calls=%async_computation.4 | async-start | bytes 4866048 | tf_op jit(solution)/shard_map/all_gather | solution.py:590
  16.3 196.5 %all-gather.8.cloned.1.call-start = ((), (), s32[]{:S(2)}) async-start(), calls=%async_computation.5 | async-start | bytes 4866048 | tf_op jit(solution)/shard_map/all_gather | solution.py:591
  17.1 363.4 %reduce-scatter.6.cloned.1.call-start = ((), (), s32[]{:S(2)}) async-start(), calls=%async_computation.6 | async-start | bytes 4866048 | tf_op jit(solution)/shard_map/reduce_scatter | solution.py:616
  274.5 218.1 %reduce-scatter.8.cloned.1.call-start = ((), (), s32[]{:S(2)}) async-start(), calls=%async_computation.7 | async-start | bytes 4866048 | tf_op jit(solution)/shard_map/reduce_scatter | solution.py:616
  275.1 323.0 %reduce-scatter.10.cloned.1.call-start = ((), (), s32[]{:S(2)}) async-start(), calls=%async_computation.8 | async-start | bytes 5068800
  276.4 70.2 %copy-start.1 = (f32[8,768]{1,0:T(8,128)S(1)}, f32[8,768]{1,0:T(8,128)}, u32[]{:S(2)}) copy-start(f32[8,768]{1,0:T(8,128)} %get-tuple-element.51) | copy-start | bytes 73732
  345.0 2.5 copy-start.2
  345.0 3.0 copy-start
Sparse Core Ops, SparseCore 0:
  15.7 66.9 all-gather.3
  85.6 61.9 all-gather.5
  150.5 62.2 all-gather.7
  274.6 105.8 reduce-scatter.5
  385.8 106.7 reduce-scatter.7
  498.1 99.8 reduce-scatter.9
